TPU v7x, 512 devices: a whole 4x4x16 slice. The times are simulated.
512 devices in a mesh: req: 16 (over x, y_lo, core), blk: 32 (over z, y_hi).
Axes of the slice: x: 4, y: 4 (y_hi: 2, y_lo: 2; y = y_hi * 2 + y_lo), z: 16, core: 2. Of those that a mesh axis runs over, the one named last changes fastest.
Arguments:
- queries: bfloat16 [16, 32, 512, 512], P('req', 'blk'), may hold values from -6 to 6
- keys: bfloat16 [16, 32, 512, 256], P('req', 'blk'), may hold values from -25 to 25
- values: bfloat16 [16, 32, 512, 256], P('req', 'blk'), may hold values from -6 to 6
- block_map: int32 [16, 8, 2], P('req'), may hold values from 0 to 15, as said below
- lengths: int32 [16], P('req'), may hold values from 1024 to 4096
- group_of_prompt: int32 [16], replicated, may hold values from 0 to 15, each once
- decode_rank: int32 [16, 32], P('req'), may hold values from 0 to 31, as said below
Outputs:
- attended: bfloat16 [16, 32, 512, 512], P('req', 'blk')
- cache: bfloat16 [16, 4096, 2048], P('req', 'blk')
Inputs may be any that keep to these rules, and one draw needn't show every extreme that they name: In each group, block_map[g] holds each of 0 to 15 once, and the two halves of each slot hold blocks b and 15 - b, in either order. `decode_rank`: each group's row holds each of 0 to 31 once.
All inputs are finite; a program needn't handle non-finite values.
Results may differ from a plain program's by a relative error of at most 0.0098.
Values may be sent and summed in bfloat16 or wider, within the bound.
A program may use at most 64 MiB of HBM per device.

v0:
```python
import math
import jax
import jax.numpy as jnp
from jax import lax
from jax.sharding import PartitionSpec as P

QUERY_HEADS = 16
KEY_VALUE_HEADS = 8
HEAD_SIZE = 128
HEAD_DIVISIONS = 4
Q_DEV = 4
KV_DEV = 2
cap_value = 50.0
query_scale = 1.0 / 12.0
rope_base = 10000.0


def shifted(shard, axis, by):
    peers = lax.axis_size(axis)
    return lax.ppermute(shard, axis, [(i, (i + by) % peers) for i in range(peers)])


def apply_rotary(row_block, token_position, head_count):
    row_count = row_block.shape[0]
    head_width = row_block.shape[1] // head_count
    half_width = head_width // 2
    shaped = row_block.astype(jnp.float32).reshape(row_count, head_count, head_width)
    frequency = jnp.exp(
        -math.log(rope_base) * (2.0 * jnp.arange(half_width, dtype=jnp.float32)) / head_width
    )
    angles = token_position.astype(jnp.float32)[:, None] * frequency[None, :]
    cosine = jnp.cos(angles)[:, None, :]
    sine_part = jnp.sin(angles)[:, None, :]
    front_half = shaped[:, :, :half_width]
    second = shaped[:, :, half_width:]
    turned = jnp.concatenate(
        [front_half * cosine - second * sine_part, second * cosine + front_half * sine_part], axis=2
    )
    return turned.reshape(row_count, head_count * head_width)


def slot_positions(table, slot, block_len):
    slot_ids = jnp.arange(table.shape[0], dtype=jnp.int32)
    chosen = jnp.sum(jnp.where((slot_ids == slot)[:, None], table, 0), axis=0)
    return chosen[:, None] * block_len + jnp.arange(block_len, dtype=jnp.int32)[None, :]


def forward_step(buffer):
    return shifted(buffer, "blk", HEAD_DIVISIONS)


def on_device(queries, keys, values, block_map, lengths, group_of_prompt, decode_rank):
    token_rows = queries.shape[2]
    block_len = token_rows // 2
    rank_count = lax.axis_size("blk")
    cache_slot_count = rank_count // HEAD_DIVISIONS
    member = lax.axis_index("blk")
    own_slot = member // HEAD_DIVISIONS
    group_id = lax.axis_index("req")
    group_portion = QUERY_HEADS // KEY_VALUE_HEADS
    kv_dev_width = KV_DEV * HEAD_SIZE
    all_lengths = lax.all_gather(lengths, "req", axis=0, tiled=True)
    length = jnp.sum(jnp.where(group_of_prompt == group_id, all_lengths, 0))
    table = block_map[0]
    own_pos = slot_positions(table, own_slot, block_len)
    flat_pos = own_pos.reshape(-1)
    query_rot = (apply_rotary(queries[0, 0], flat_pos, Q_DEV) * query_scale).astype(jnp.bfloat16)
    rotated_key = apply_rotary(keys[0, 0], flat_pos, KV_DEV).astype(jnp.bfloat16)
    value_row_list = values[0, 0]
    query_halves = query_rot.reshape(2, block_len, KV_DEV, group_portion, HEAD_SIZE)

    def attend_tile(numerator, denominator, portion, key_sub, value_sub, key_pos):
        scores = jnp.einsum(
            "qkgd,nkd->kgqn", query_halves[portion], key_sub, preferred_element_type=jnp.float32
        )
        capped = cap_value * jnp.tanh(scores / cap_value)
        allowed = key_pos[None, :] <= own_pos[portion][:, None]
        expo_vals = jnp.where(allowed[None, None], jnp.exp(capped), 0.0)
        weight = expo_vals.astype(jnp.bfloat16)
        numerator = numerator + jnp.einsum(
            "kgqn,nkd->qkgd", weight, value_sub, preferred_element_type=jnp.float32
        )
        denominator = denominator + jnp.sum(expo_vals, axis=3)
        return (numerator, denominator)

    def absorb(totals, packet, slot):
        numerator, denominator = totals
        key_pos = slot_positions(table, slot, block_len)
        key_blocks = packet[0].reshape(2, block_len, KV_DEV, HEAD_SIZE)
        value_blocks = packet[1].reshape(2, block_len, KV_DEV, HEAD_SIZE)
        new_numer = []
        new_denom = []
        for portion in range(2):
            result_pair = (numerator[portion], denominator[portion])
            for half in range(2):
                result_pair = attend_tile(
                    result_pair[0],
                    result_pair[1],
                    portion,
                    key_blocks[half],
                    value_blocks[half],
                    key_pos[half],
                )
            new_numer.append(result_pair[0])
            new_denom.append(result_pair[1])
        return (jnp.stack(new_numer), jnp.stack(new_denom))

    packet = jnp.stack([rotated_key, value_row_list])
    start_numer = jnp.zeros((2, block_len, KV_DEV, group_portion, HEAD_SIZE), jnp.float32)
    start_denom = jnp.zeros((2, KV_DEV, group_portion, block_len), jnp.float32)
    numerator, denominator = absorb((start_numer, start_denom), packet, own_slot)

    def step_single(turn, carry):
        numer_now, denom_now, buffer = carry
        buffer = forward_step(buffer)
        numer_now, denom_now = absorb(
            (numer_now, denom_now), buffer, (own_slot - turn) % cache_slot_count
        )
        return (numer_now, denom_now, buffer)

    numerator, denominator, _ = lax.fori_loop(
        1, cache_slot_count, step_single, (numerator, denominator, packet)
    )
    safe_denom = jnp.where(denominator > 0.0, denominator, 1.0)
    output = numerator / jnp.transpose(safe_denom, (0, 3, 1, 2))[..., None]
    output = output.reshape(token_rows, Q_DEV * HEAD_SIZE)
    live = flat_pos < length
    attended = jnp.where(live[:, None], output, 0.0).astype(jnp.bfloat16)
    joined = jnp.concatenate([rotated_key, value_row_list], axis=1)
    kept_rows = jnp.where(live[:, None], joined, jnp.zeros_like(joined))
    rank_portion = block_len // rank_count
    shaped = kept_rows.reshape(2, rank_portion, rank_count, 2 * kv_dev_width)
    rank_of = decode_rank[0]
    rank_ids = jnp.arange(rank_count, dtype=jnp.int32)
    inverse = jnp.sum(
        jnp.where(rank_of[None, :] == rank_ids[:, None], rank_ids[None, :], 0), axis=1
    )
    outgoing = jnp.take(shaped, inverse, axis=2)
    arrived = lax.all_to_all(outgoing, "blk", split_axis=2, concat_axis=2, tiled=True)
    regrouped = arrived.reshape(2, rank_portion, cache_slot_count, HEAD_DIVISIONS, 2, kv_dev_width)
    regrouped = jnp.transpose(regrouped, (2, 0, 1, 4, 3, 5)).reshape(
        cache_slot_count * 2 * rank_portion, 2 * KEY_VALUE_HEADS * HEAD_SIZE
    )
    target = (
        table.reshape(-1)[:, None] * rank_portion
        + jnp.arange(rank_portion, dtype=jnp.int32)[None, :]
    )
    cache_rows = (
        jnp.zeros((token_rows // HEAD_DIVISIONS, 2 * KEY_VALUE_HEADS * HEAD_SIZE), jnp.bfloat16)
        .at[target.reshape(-1)]
        .set(regrouped)
    )
    return (attended[None, None], cache_rows[None])


def solution(mesh):
    placed = (
        P("req", "blk", None, None),
        P("req", "blk", None, None),
        P("req", "blk", None, None),
        P("req", None, None),
        P("req"),
        P(),
        P("req", None),
    )
    return jax.shard_map(
        on_device,
        mesh=mesh,
        in_specs=placed,
        out_specs=(P("req", "blk", None, None), P("req", "blk", None)),
        check_vma=False,
    )
```

profile of v0, /device:TPU:16, one launch (start us, length us, event | category | flops | bytes accessed | tf_op | source)
XLA Modules:
  0.0 276.7 jit_solution(10896126467494985319)
XLA Ops:
  0.7 0.6 copy-done.4
  1.5 0.7 copy-done.2
  2.3 1.1 copy.148
  3.9 0.5 multiply_cosine_fusion
  5.4 1.3 dynamic-slice
  6.7 0.8 dynamic-update-slice
  7.4 12.1 %all-reduce = s32[16]{0:T(128)S(1)} all-reduce(s32[16]{0:T(128)S(1)} %dynamic-update-slice), channel_id=1, replica_groups=mesh['req'=16,'blk'=32] {'req'}, use_global_device_ids=true, to_apply=%add | all-reduce | flops 16 | bytes 128
  20.6 0.5 copy-done.3
  21.1 0.6 fusion.71
  21.7 0.6 add_compare_fusion
  22.6 0.6 gather_fusion
  23.2 0.9 select_bitcast_fusion
  24.1 18.2 %all-to-all-start = ((bf16[2,8,32,512]{3,1,0,2:T(8,128)(2,1)}), bf16[2,8,32,512]{3,1,0,2:T(8,128)(2,1)S(1)}, u32[]{:S(2)}, u32[]{:S(2)}) async-start(bf16[2,8,32,512]{3,1,0,2:T(8,128)(2,1)} %select_bitcast_fusion), calls=%async_computation | async-start | bytes 1048576 | tf_op jit(solution)/shard_map/all_to_all | solution.py:139
  42.6 0.7 copy-done.1
  44.6 0.5 fusion.85
  45.9 0.5 fusion.87
  48.2 222.1 %while.19 = (s32[]{:T(128)}, f32[2,256,2,2,128]{4,1,3,2,0:T(8,128)S(1)}, f32[2,2,2,256]{3,2,1,0:T(2,128)S(1)}, bf16[2,512,256]{1,2,0:T(8,128)(2,1)S(1)}, s32[]{:...) while((s32[]{:T(128)}, ...), condition=%wide.region_12.13_spmd, body=%wide.region_6.0_spmd.sunk | while | flops 543164992 | bytes 17381768 | solution.py:121
  48.2 4.3 %collective-permute-start = (bf16[2,512,256]{1,2,0:T(8,128)(2,1)S(1)}, bf16[2,512,256]{1,2,0:T(8,128)(2,1)S(1)}, u32[]{:S(2)}, u32[]{:S(2)}) collective-permute-start(bf16[2,512,256]{1,2,0:T(8,128)(2,1)S(1)} %get-tuple-element.428), channel_id=1, source_target_pairs={{0,4},{1,5},{2,6},{3,7},{4,8},{5,9},{6,10},{7,11},{8,12},{9,13},{1... | collective-permute-start | bytes 1572872 | tf_op jit(solution)/shard_map/while/body/eval_jaxpr/ppermute | solution.py:20
  52.9 31.1 %collective-permute-done = bf16[2,512,256]{1,2,0:T(8,128)(2,1)S(1)} collective-permute-done((bf16[2,512,256]{1,2,0:T(8,128)(2,1)S(1)}, bf16[2,512,256]{1,2,0:T(8,128)(2,1)S(1)}, u32[]{:S(2)}, u32[]{:S(2)}) %collective-permute-start) | collective-permute-done | bytes 524320 | tf_op jit(solution)/shard_map/while/body/eval_jaxpr/ppermute | solution.py:20
  84.1 0.5 fusion.149
  84.7 0.5 fusion.152
  85.9 0.5 fusion.150
  86.4 0.5 fusion.153
  87.9 1.9 collective-permute-start
  90.3 17.8 %collective-permute-done = bf16[2,512,256]{1,2,0:T(8,128)(2,1)S(1)} collective-permute-done((bf16[2,512,256]{1,2,0:T(8,128)(2,1)S(1)}, bf16[2,512,256]{1,2,0:T(8,128)(2,1)S(1)}, u32[]{:S(2)}, u32[]{:S(2)}) %collective-permute-start) | collective-permute-done | bytes 524320 | tf_op jit(solution)/shard_map/while/body/eval_jaxpr/ppermute | solution.py:20
  108.1 0.5 fusion.149
  108.7 0.5 fusion.152
  109.9 0.5 fusion.150
  110.5 0.5 fusion.153
  111.9 8.9 %collective-permute-start = (bf16[2,512,256]{1,2,0:T(8,128)(2,1)S(1)}, bf16[2,512,256]{1,2,0:T(8,128)(2,1)S(1)}, u32[]{:S(2)}, u32[]{:S(2)}) collective-permute-start(bf16[2,512,256]{1,2,0:T(8,128)(2,1)S(1)} %get-tuple-element.428), channel_id=1, source_target_pairs={{0,4},{1,5},{2,6},{3,7},{4,8},{5,9},{6,10},{7,11},{8,12},{9,13},{1... | collective-permute-start | bytes 1572872 | tf_op jit(solution)/shard_map/while/body/eval_jaxpr/ppermute | solution.py:20
  121.3 19.4 %collective-permute-done = bf16[2,512,256]{1,2,0:T(8,128)(2,1)S(1)} collective-permute-done((bf16[2,512,256]{1,2,0:T(8,128)(2,1)S(1)}, bf16[2,512,256]{1,2,0:T(8,128)(2,1)S(1)}, u32[]{:S(2)}, u32[]{:S(2)}) %collective-permute-start) | collective-permute-done | bytes 524320 | tf_op jit(solution)/shard_map/while/body/eval_jaxpr/ppermute | solution.py:20
  140.7 0.5 fusion.149
  141.3 0.5 fusion.152
  142.5 0.5 fusion.150
  143.1 0.5 fusion.153
  144.5 8.8 %collective-permute-start = (bf16[2,512,256]{1,2,0:T(8,128)(2,1)S(1)}, bf16[2,512,256]{1,2,0:T(8,128)(2,1)S(1)}, u32[]{:S(2)}, u32[]{:S(2)}) collective-permute-start(bf16[2,512,256]{1,2,0:T(8,128)(2,1)S(1)} %get-tuple-element.428), channel_id=1, source_target_pairs={{0,4},{1,5},{2,6},{3,7},{4,8},{5,9},{6,10},{7,11},{8,12},{9,13},{1... | collective-permute-start | bytes 1572872 | tf_op jit(solution)/shard_map/while/body/eval_jaxpr/ppermute | solution.py:20
  153.8 17.7 %collective-permute-done = bf16[2,512,256]{1,2,0:T(8,128)(2,1)S(1)} collective-permute-done((bf16[2,512,256]{1,2,0:T(8,128)(2,1)S(1)}, bf16[2,512,256]{1,2,0:T(8,128)(2,1)S(1)}, u32[]{:S(2)}, u32[]{:S(2)}) %collective-permute-start) | collective-permute-done | bytes 524320 | tf_op jit(solution)/shard_map/while/body/eval_jaxpr/ppermute | solution.py:20
  171.5 0.5 fusion.149
  172.1 0.5 fusion.152
  173.3 0.5 fusion.150
  173.8 0.5 fusion.153
  175.3 9.2 %collective-permute-start = (bf16[2,512,256]{1,2,0:T(8,128)(2,1)S(1)}, bf16[2,512,256]{1,2,0:T(8,128)(2,1)S(1)}, u32[]{:S(2)}, u32[]{:S(2)}) collective-permute-start(bf16[2,512,256]{1,2,0:T(8,128)(2,1)S(1)} %get-tuple-element.428), channel_id=1, source_target_pairs={{0,4},{1,5},{2,6},{3,7},{4,8},{5,9},{6,10},{7,11},{8,12},{9,13},{1... | collective-permute-start | bytes 1572872 | tf_op jit(solution)/shard_map/while/body/eval_jaxpr/ppermute | solution.py:20
  185.0 21.1 %collective-permute-done = bf16[2,512,256]{1,2,0:T(8,128)(2,1)S(1)} collective-permute-done((bf16[2,512,256]{1,2,0:T(8,128)(2,1)S(1)}, bf16[2,512,256]{1,2,0:T(8,128)(2,1)S(1)}, u32[]{:S(2)}, u32[]{:S(2)}) %collective-permute-start) | collective-permute-done | bytes 524320 | tf_op jit(solution)/shard_map/while/body/eval_jaxpr/ppermute | solution.py:20
  206.1 0.5 fusion.149
  206.7 0.5 fusion.152
  207.9 0.5 fusion.150
  208.5 0.5 fusion.153
  209.9 6.5 %collective-permute-start = (bf16[2,512,256]{1,2,0:T(8,128)(2,1)S(1)}, bf16[2,512,256]{1,2,0:T(8,128)(2,1)S(1)}, u32[]{:S(2)}, u32[]{:S(2)}) collective-permute-start(bf16[2,512,256]{1,2,0:T(8,128)(2,1)S(1)} %get-tuple-element.428), channel_id=1, source_target_pairs={{0,4},{1,5},{2,6},{3,7},{4,8},{5,9},{6,10},{7,11},{8,12},{9,13},{1... | collective-permute-start | bytes 1572872 | tf_op jit(solution)/shard_map/while/body/eval_jaxpr/ppermute | solution.py:20
  216.9 32.6 %collective-permute-done = bf16[2,512,256]{1,2,0:T(8,128)(2,1)S(1)} collective-permute-done((bf16[2,512,256]{1,2,0:T(8,128)(2,1)S(1)}, bf16[2,512,256]{1,2,0:T(8,128)(2,1)S(1)}, u32[]{:S(2)}, u32[]{:S(2)}) %collective-permute-start) | collective-permute-done | bytes 524320 | tf_op jit(solution)/shard_map/while/body/eval_jaxpr/ppermute | solution.py:20
  249.6 0.5 fusion.149
  250.1 0.5 fusion.152
  251.4 0.5 fusion.150
  251.9 0.5 fusion.153
  253.3 5.3 %collective-permute-start = (bf16[2,512,256]{1,2,0:T(8,128)(2,1)S(1)}, bf16[2,512,256]{1,2,0:T(8,128)(2,1)S(1)}, u32[]{:S(2)}, u32[]{:S(2)}) collective-permute-start(bf16[2,512,256]{1,2,0:T(8,128)(2,1)S(1)} %get-tuple-element.428), channel_id=1, source_target_pairs={{0,4},{1,5},{2,6},{3,7},{4,8},{5,9},{6,10},{7,11},{8,12},{9,13},{1... | collective-permute-start | bytes 1572872 | tf_op jit(solution)/shard_map/while/body/eval_jaxpr/ppermute | solution.py:20
  259.1 7.4 %collective-permute-done = bf16[2,512,256]{1,2,0:T(8,128)(2,1)S(1)} collective-permute-done((bf16[2,512,256]{1,2,0:T(8,128)(2,1)S(1)}, bf16[2,512,256]{1,2,0:T(8,128)(2,1)S(1)}, u32[]{:S(2)}, u32[]{:S(2)}) %collective-permute-start) | collective-permute-done | bytes 524320 | tf_op jit(solution)/shard_map/while/body/eval_jaxpr/ppermute | solution.py:20
  266.5 0.5 fusion.149
  267.1 0.5 fusion.152
  268.3 0.5 fusion.150
  268.9 0.5 fusion.153
  270.7 0.5 copy.170
  271.4 0.6 fusion.70
  272.4 1.0 select_convert_fusion
  273.5 0.7 copy.176
  274.6 2.1 scatter_custom_fusion
  (176 shorter events, 21.6 us)
Async XLA Ops:
  0.7 0.7 copy-start.4
  1.5 0.7 copy-start.2
  4.6 15.0 %copy-start = (bf16[1,1,512,256]{3,2,1,0:T(8,128)(2,1)S(1)}, bf16[1,1,512,256]{3,2,1,0:T(8,128)(2,1)}, u32[]{:S(2)}) copy-start(bf16[1,1,512,256]{3,2,1,0:T(8,128)(2,1)} %param.11) | copy-start | bytes 786436
  20.5 0.7 copy-start.3
  24.1 249.3 %all-to-all-start = ((bf16[2,8,32,512]{3,1,0,2:T(8,128)(2,1)}), bf16[2,8,32,512]{3,1,0,2:T(8,128)(2,1)S(1)}, u32[]{:S(2)}, u32[]{:S(2)}) async-start(bf16[2,8,32,512]{3,1,0,2:T(8,128)(2,1)} %select_bitcast_fusion), calls=%async_computation | async-start | bytes 1048576 | tf_op jit(solution)/shard_map/all_to_all | solution.py:139
  42.3 1.0 copy-start.1
  48.2 35.9 %collective-permute-start = (bf16[2,512,256]{1,2,0:T(8,128)(2,1)S(1)}, bf16[2,512,256]{1,2,0:T(8,128)(2,1)S(1)}, u32[]{:S(2)}, u32[]{:S(2)}) collective-permute-start(bf16[2,512,256]{1,2,0:T(8,128)(2,1)S(1)} %get-tuple-element.428), channel_id=1, source_target_pairs={{0,4},{1,5},{2,6},{3,7},{4,8},{5,9},{6,10},{7,11},{8,12},{9,13},{1... | collective-permute-start | bytes 1572872 | tf_op jit(solution)/shard_map/while/body/eval_jaxpr/ppermute | solution.py:20
  87.9 20.2 %collective-permute-start = (bf16[2,512,256]{1,2,0:T(8,128)(2,1)S(1)}, bf16[2,512,256]{1,2,0:T(8,128)(2,1)S(1)}, u32[]{:S(2)}, u32[]{:S(2)}) collective-permute-start(bf16[2,512,256]{1,2,0:T(8,128)(2,1)S(1)} %get-tuple-element.428), channel_id=1, source_target_pairs={{0,4},{1,5},{2,6},{3,7},{4,8},{5,9},{6,10},{7,11},{8,12},{9,13},{1... | collective-permute-start | bytes 1572872 | tf_op jit(solution)/shard_map/while/body/eval_jaxpr/ppermute | solution.py:20
  111.9 28.8 %collective-permute-start = (bf16[2,512,256]{1,2,0:T(8,128)(2,1)S(1)}, bf16[2,512,256]{1,2,0:T(8,128)(2,1)S(1)}, u32[]{:S(2)}, u32[]{:S(2)}) collective-permute-start(bf16[2,512,256]{1,2,0:T(8,128)(2,1)S(1)} %get-tuple-element.428), channel_id=1, source_target_pairs={{0,4},{1,5},{2,6},{3,7},{4,8},{5,9},{6,10},{7,11},{8,12},{9,13},{1... | collective-permute-start | bytes 1572872 | tf_op jit(solution)/shard_map/while/body/eval_jaxpr/ppermute | solution.py:20
  144.5 27.0 %collective-permute-start = (bf16[2,512,256]{1,2,0:T(8,128)(2,1)S(1)}, bf16[2,512,256]{1,2,0:T(8,128)(2,1)S(1)}, u32[]{:S(2)}, u32[]{:S(2)}) collective-permute-start(bf16[2,512,256]{1,2,0:T(8,128)(2,1)S(1)} %get-tuple-element.428), channel_id=1, source_target_pairs={{0,4},{1,5},{2,6},{3,7},{4,8},{5,9},{6,10},{7,11},{8,12},{9,13},{1... | collective-permute-start | bytes 1572872 | tf_op jit(solution)/shard_map/while/body/eval_jaxpr/ppermute | solution.py:20
  175.3 30.8 %collective-permute-start = (bf16[2,512,256]{1,2,0:T(8,128)(2,1)S(1)}, bf16[2,512,256]{1,2,0:T(8,128)(2,1)S(1)}, u32[]{:S(2)}, u32[]{:S(2)}) collective-permute-start(bf16[2,512,256]{1,2,0:T(8,128)(2,1)S(1)} %get-tuple-element.428), channel_id=1, source_target_pairs={{0,4},{1,5},{2,6},{3,7},{4,8},{5,9},{6,10},{7,11},{8,12},{9,13},{1... | collective-permute-start | bytes 1572872 | tf_op jit(solution)/shard_map/while/body/eval_jaxpr/ppermute | solution.py:20
  209.9 39.7 %collective-permute-start = (bf16[2,512,256]{1,2,0:T(8,128)(2,1)S(1)}, bf16[2,512,256]{1,2,0:T(8,128)(2,1)S(1)}, u32[]{:S(2)}, u32[]{:S(2)}) collective-permute-start(bf16[2,512,256]{1,2,0:T(8,128)(2,1)S(1)} %get-tuple-element.428), channel_id=1, source_target_pairs={{0,4},{1,5},{2,6},{3,7},{4,8},{5,9},{6,10},{7,11},{8,12},{9,13},{1... | collective-permute-start | bytes 1572872 | tf_op jit(solution)/shard_map/while/body/eval_jaxpr/ppermute | solution.py:20
  253.3 13.2 %collective-permute-start = (bf16[2,512,256]{1,2,0:T(8,128)(2,1)S(1)}, bf16[2,512,256]{1,2,0:T(8,128)(2,1)S(1)}, u32[]{:S(2)}, u32[]{:S(2)}) collective-permute-start(bf16[2,512,256]{1,2,0:T(8,128)(2,1)S(1)} %get-tuple-element.428), channel_id=1, source_target_pairs={{0,4},{1,5},{2,6},{3,7},{4,8},{5,9},{6,10},{7,11},{8,12},{9,13},{1... | collective-permute-start | bytes 1572872 | tf_op jit(solution)/shard_map/while/body/eval_jaxpr/ppermute | solution.py:20
where the time goes:
time: 277 us
  waiting for transfers between devices  147 us (53%)
  starting transfers between devices  63.2 us (23%)
  matrix products  28.1 us (10%)
  local copies, waits for them, and re-layouts  13.5 us (5%)
  blocking collectives  12.1 us (4%)
  other arithmetic  9.92 us (4%)
    ppermute x7, waiting for transfers between devices, shifted(): lax.ppermute(shard, axis, [(i, (i + by) % peers) for i in range(peers)])  147 us
    ppermute x7, starting transfers between devices, shifted(): lax.ppermute(shard, axis, [(i, (i + by) % peers) for i in range(peers)])  45 us
    all_to_all x1, starting transfers between devices, on_device(): lax.all_to_all(outgoing, 'blk', split_axis=2, concat_axis=2, tiled=True)  18.2 us
    dot_general x32, matrix products, attend_tile(): jnp.einsum('qkgd,nkd->kgqn', query_halves[portion], key_sub, preferred_el...  17 us
    unnamed x1, blocking collectives  12.1 us
    dot_general x32, matrix products, attend_tile(): jnp.einsum('kgqn,nkd->qkgd', weight, value_sub, preferred_element_type=jn...  11.1 us
    unnamed x19, local copies, waits for them, and re-layouts  6.42 us
  transfers between devices with their start and end apart: 8, of which 7 were waited for; matrix products, arithmetic and copies ran while one was open for 13% of the time, Pallas kernels for 0%

commit v1 on v0

--- a/solution.py
+++ b/solution.py
@@ -1,3 +1,4 @@
+import functools
 import math
 import jax
 import jax.numpy as jnp
@@ -13,6 +14,18 @@
 cap_value = 50.0
 query_scale = 1.0 / 12.0
 rope_base = 10000.0
+
+
+def store_tails_over_axis(local_x, axis_tag):
+    return jnp.concatenate(
+        lax.all_to_all(
+            jnp.stack(jnp.split(local_x, lax.psum(1, axis_tag), axis=2), axis=0), axis_tag, 0, 0
+        ),
+        axis=2,
+    )
+
+
+press_digits_all = functools.partial(store_tails_over_axis, axis_tag="blk")
 
 
 def shifted(shard, axis, by):
@@ -136,7 +149,7 @@
         jnp.where(rank_of[None, :] == rank_ids[:, None], rank_ids[None, :], 0), axis=1
     )
     outgoing = jnp.take(shaped, inverse, axis=2)
-    arrived = lax.all_to_all(outgoing, "blk", split_axis=2, concat_axis=2, tiled=True)
+    arrived = press_digits_all(outgoing)
     regrouped = arrived.reshape(2, rank_portion, cache_slot_count, HEAD_DIVISIONS, 2, kv_dev_width)
     regrouped = jnp.transpose(regrouped, (2, 0, 1, 4, 3, 5)).reshape(
         cache_slot_count * 2 * rank_portion, 2 * KEY_VALUE_HEADS * HEAD_SIZE

time: 277 us -> 296 us (1.069)
  the two profiles are of different devices: /device:TPU:16 before, /device:TPU:130 now
where the time goes in v1:
time: 296 us; the launch traced here: 295 us
  waiting for transfers between devices  149 us (50%)
  starting transfers between devices  62.1 us (21%)
  local copies, waits for them, and re-layouts  32.9 us (11%)
  matrix products  28.1 us (9%)
  blocking collectives  11.1 us (4%)
  other arithmetic  9.12 us (3%)
    ppermute x7, waiting for transfers between devices, shifted(): lax.ppermute(shard, axis, [(i, (i + by) % peers) for i in range(peers)])  149 us
    ppermute x7, starting transfers between devices, shifted(): lax.ppermute(shard, axis, [(i, (i + by) % peers) for i in range(peers)])  45.7 us
    unnamed x50, local copies, waits for them, and re-layouts  25.2 us
    dot_general x32, matrix products, attend_tile(): jnp.einsum('qkgd,nkd->kgqn', query_halves[portion], key_sub, preferred_el...  17 us
    all_to_all x1, starting transfers between devices, store_tails_over_axis(): lax.all_to_all(jnp.stack(jnp.split(local_x, lax.psum(1, axis_tag), axis=2...  16.3 us
    unnamed x1, blocking collectives  11.1 us
    dot_general x32, matrix products, attend_tile(): jnp.einsum('kgqn,nkd->qkgd', weight, value_sub, preferred_element_type=jn...  11.1 us
  transfers between devices with their start and end apart: 8, of which 7 were waited for; matrix products, arithmetic and copies ran while one was open for 13% of the time, Pallas kernels for 0%

profile of v1, /device:TPU:130, one launch (start us, length us, event | category | flops | bytes accessed | tf_op | source)
XLA Modules:
  0.0 295.3 jit_solution(10119930460342370033)
XLA Ops:
  0.7 0.6 copy-done.4
  1.5 0.7 copy-done.2
  2.3 1.1 copy.179
  5.4 1.3 dynamic-slice
  6.7 0.8 dynamic-update-slice
  7.4 11.1 %all-reduce = s32[16]{0:T(128)S(1)} all-reduce(s32[16]{0:T(128)S(1)} %dynamic-update-slice), channel_id=1, replica_groups=mesh['req'=16,'blk'=32] {'req'}, use_global_device_ids=true, to_apply=%add | all-reduce | flops 16 | bytes 128
  20.1 0.6 fusion.71
  20.8 0.6 add_compare_fusion
  21.6 0.6 gather_fusion
  22.3 0.6 constant_dynamic-update-slice_fusion.31
  22.9 0.6 constant_dynamic-update-slice_fusion.30
  23.5 0.6 constant_dynamic-update-slice_fusion.29
  24.1 0.6 constant_dynamic-update-slice_fusion.28
  24.7 0.6 constant_dynamic-update-slice_fusion.27
  25.3 0.6 constant_dynamic-update-slice_fusion.26
  25.9 0.6 constant_dynamic-update-slice_fusion.25
  26.5 0.6 constant_dynamic-update-slice_fusion.24
  27.1 0.6 constant_dynamic-update-slice_fusion.23
  27.8 0.6 constant_dynamic-update-slice_fusion.22
  28.4 0.6 constant_dynamic-update-slice_fusion.21
  29.0 0.6 constant_dynamic-update-slice_fusion.20
  29.6 0.6 constant_dynamic-update-slice_fusion.19
  30.2 0.6 constant_dynamic-update-slice_fusion.18
  30.8 0.6 constant_dynamic-update-slice_fusion.17
  31.4 0.6 constant_dynamic-update-slice_fusion.16
  32.0 0.6 constant_dynamic-update-slice_fusion.15
  32.6 0.6 constant_dynamic-update-slice_fusion.14
  33.2 0.6 constant_dynamic-update-slice_fusion.13
  33.8 0.6 constant_dynamic-update-slice_fusion.12
  34.4 0.6 constant_dynamic-update-slice_fusion.11
  35.0 0.6 constant_dynamic-update-slice_fusion.10
  35.6 0.6 constant_dynamic-update-slice_fusion.9
  36.3 0.6 constant_dynamic-update-slice_fusion.8
  36.9 0.6 constant_dynamic-update-slice_fusion.7
  37.5 0.6 constant_dynamic-update-slice_fusion.6
  38.1 0.6 constant_dynamic-update-slice_fusion.5
  38.7 0.6 constant_dynamic-update-slice_fusion.4
  39.3 0.6 constant_dynamic-update-slice_fusion.3
  39.9 0.6 constant_dynamic-update-slice_fusion.2
  40.5 0.6 constant_dynamic-update-slice_fusion.1
  41.1 0.6 constant_dynamic-update-slice_fusion
  41.7 16.3 %all-to-all-start = ((bf16[32,2,8,1,512]{4,2,1,3,0:T(8,128)(2,1)}), bf16[32,2,8,1,512]{4,2,1,3,0:T(8,128)(2,1)S(1)}, u32[]{:S(2)}, u32[]{:S(2)}) async-start(bf16[32,2,8,1,512]{4,2,1,3,0:T(8,128)(2,1)} %constant_dynamic-update-slice_fusion), calls=%async_computation | async-start | bytes 1048576 | tf_op jit(solution)/shard_map/all_to_all | solution.py:21
  58.4 0.7 copy-done.1
  63.9 224.9 %while.19 = (s32[]{:T(128)}, f32[2,256,2,2,128]{4,1,3,2,0:T(8,128)S(1)}, f32[2,2,2,256]{3,2,1,0:T(2,128)S(1)}, bf16[2,512,256]{1,2,0:T(8,128)(2,1)S(1)}, s32[]{:...) while((s32[]{:T(128)}, ...), condition=%wide.region_12.13_spmd, body=%wide.region_6.0_spmd.sunk | while | flops 543164992 | bytes 17381768 | solution.py:134
  63.9 4.3 %collective-permute-start = (bf16[2,512,256]{1,2,0:T(8,128)(2,1)S(1)}, bf16[2,512,256]{1,2,0:T(8,128)(2,1)S(1)}, u32[]{:S(2)}, u32[]{:S(2)}) collective-permute-start(bf16[2,512,256]{1,2,0:T(8,128)(2,1)S(1)} %get-tuple-element.428), channel_id=1, source_target_pairs={{0,4},{1,5},{2,6},{3,7},{4,8},{5,9},{6,10},{7,11},{8,12},{9,13},{1... | collective-permute-start | bytes 1572872 | tf_op jit(solution)/shard_map/while/body/eval_jaxpr/ppermute | solution.py:33
  68.7 28.3 %collective-permute-done = bf16[2,512,256]{1,2,0:T(8,128)(2,1)S(1)} collective-permute-done((bf16[2,512,256]{1,2,0:T(8,128)(2,1)S(1)}, bf16[2,512,256]{1,2,0:T(8,128)(2,1)S(1)}, u32[]{:S(2)}, u32[]{:S(2)}) %collective-permute-start) | collective-permute-done | bytes 524320 | tf_op jit(solution)/shard_map/while/body/eval_jaxpr/ppermute | solution.py:33
  99.3 0.5 fusion.153
  100.7 4.3 %collective-permute-start = (bf16[2,512,256]{1,2,0:T(8,128)(2,1)S(1)}, bf16[2,512,256]{1,2,0:T(8,128)(2,1)S(1)}, u32[]{:S(2)}, u32[]{:S(2)}) collective-permute-start(bf16[2,512,256]{1,2,0:T(8,128)(2,1)S(1)} %get-tuple-element.428), channel_id=1, source_target_pairs={{0,4},{1,5},{2,6},{3,7},{4,8},{5,9},{6,10},{7,11},{8,12},{9,13},{1... | collective-permute-start | bytes 1572872 | tf_op jit(solution)/shard_map/while/body/eval_jaxpr/ppermute | solution.py:33
  105.5 12.6 %collective-permute-done = bf16[2,512,256]{1,2,0:T(8,128)(2,1)S(1)} collective-permute-done((bf16[2,512,256]{1,2,0:T(8,128)(2,1)S(1)}, bf16[2,512,256]{1,2,0:T(8,128)(2,1)S(1)}, u32[]{:S(2)}, u32[]{:S(2)}) %collective-permute-start) | collective-permute-done | bytes 524320 | tf_op jit(solution)/shard_map/while/body/eval_jaxpr/ppermute | solution.py:33
  120.4 0.5 fusion.153
  121.9 14.7 %collective-permute-start = (bf16[2,512,256]{1,2,0:T(8,128)(2,1)S(1)}, bf16[2,512,256]{1,2,0:T(8,128)(2,1)S(1)}, u32[]{:S(2)}, u32[]{:S(2)}) collective-permute-start(bf16[2,512,256]{1,2,0:T(8,128)(2,1)S(1)} %get-tuple-element.428), channel_id=1, source_target_pairs={{0,4},{1,5},{2,6},{3,7},{4,8},{5,9},{6,10},{7,11},{8,12},{9,13},{1... | collective-permute-start | bytes 1572872 | tf_op jit(solution)/shard_map/while/body/eval_jaxpr/ppermute | solution.py:33
  137.1 21.2 %collective-permute-done = bf16[2,512,256]{1,2,0:T(8,128)(2,1)S(1)} collective-permute-done((bf16[2,512,256]{1,2,0:T(8,128)(2,1)S(1)}, bf16[2,512,256]{1,2,0:T(8,128)(2,1)S(1)}, u32[]{:S(2)}, u32[]{:S(2)}) %collective-permute-start) | collective-permute-done | bytes 524320 | tf_op jit(solution)/shard_map/while/body/eval_jaxpr/ppermute | solution.py:33
  162.0 6.5 %collective-permute-start = (bf16[2,512,256]{1,2,0:T(8,128)(2,1)S(1)}, bf16[2,512,256]{1,2,0:T(8,128)(2,1)S(1)}, u32[]{:S(2)}, u32[]{:S(2)}) collective-permute-start(bf16[2,512,256]{1,2,0:T(8,128)(2,1)S(1)} %get-tuple-element.428), channel_id=1, source_target_pairs={{0,4},{1,5},{2,6},{3,7},{4,8},{5,9},{6,10},{7,11},{8,12},{9,13},{1... | collective-permute-start | bytes 1572872 | tf_op jit(solution)/shard_map/while/body/eval_jaxpr/ppermute | solution.py:33
  169.0 31.8 %collective-permute-done = bf16[2,512,256]{1,2,0:T(8,128)(2,1)S(1)} collective-permute-done((bf16[2,512,256]{1,2,0:T(8,128)(2,1)S(1)}, bf16[2,512,256]{1,2,0:T(8,128)(2,1)S(1)}, u32[]{:S(2)}, u32[]{:S(2)}) %collective-permute-start) | collective-permute-done | bytes 524320 | tf_op jit(solution)/shard_map/while/body/eval_jaxpr/ppermute | solution.py:33
  204.6 8.8 %collective-permute-start = (bf16[2,512,256]{1,2,0:T(8,128)(2,1)S(1)}, bf16[2,512,256]{1,2,0:T(8,128)(2,1)S(1)}, u32[]{:S(2)}, u32[]{:S(2)}) collective-permute-start(bf16[2,512,256]{1,2,0:T(8,128)(2,1)S(1)} %get-tuple-element.428), channel_id=1, source_target_pairs={{0,4},{1,5},{2,6},{3,7},{4,8},{5,9},{6,10},{7,11},{8,12},{9,13},{1... | collective-permute-start | bytes 1572872 | tf_op jit(solution)/shard_map/while/body/eval_jaxpr/ppermute | solution.py:33
  213.8 21.7 %collective-permute-done = bf16[2,512,256]{1,2,0:T(8,128)(2,1)S(1)} collective-permute-done((bf16[2,512,256]{1,2,0:T(8,128)(2,1)S(1)}, bf16[2,512,256]{1,2,0:T(8,128)(2,1)S(1)}, u32[]{:S(2)}, u32[]{:S(2)}) %collective-permute-start) | collective-permute-done | bytes 524320 | tf_op jit(solution)/shard_map/while/body/eval_jaxpr/ppermute | solution.py:33
  239.3 5.3 %collective-permute-start = (bf16[2,512,256]{1,2,0:T(8,128)(2,1)S(1)}, bf16[2,512,256]{1,2,0:T(8,128)(2,1)S(1)}, u32[]{:S(2)}, u32[]{:S(2)}) collective-permute-start(bf16[2,512,256]{1,2,0:T(8,128)(2,1)S(1)} %get-tuple-element.428), channel_id=1, source_target_pairs={{0,4},{1,5},{2,6},{3,7},{4,8},{5,9},{6,10},{7,11},{8,12},{9,13},{1... | collective-permute-start | bytes 1572872 | tf_op jit(solution)/shard_map/while/body/eval_jaxpr/ppermute | solution.py:33
  245.1 23.0 %collective-permute-done = bf16[2,512,256]{1,2,0:T(8,128)(2,1)S(1)} collective-permute-done((bf16[2,512,256]{1,2,0:T(8,128)(2,1)S(1)}, bf16[2,512,256]{1,2,0:T(8,128)(2,1)S(1)}, u32[]{:S(2)}, u32[]{:S(2)}) %collective-permute-start) | collective-permute-done | bytes 524320 | tf_op jit(solution)/shard_map/while/body/eval_jaxpr/ppermute | solution.py:33
  271.8 1.9 collective-permute-start
  274.3 10.8 %collective-permute-done = bf16[2,512,256]{1,2,0:T(8,128)(2,1)S(1)} collective-permute-done((bf16[2,512,256]{1,2,0:T(8,128)(2,1)S(1)}, bf16[2,512,256]{1,2,0:T(8,128)(2,1)S(1)}, u32[]{:S(2)}, u32[]{:S(2)}) %collective-permute-start) | collective-permute-done | bytes 524320 | tf_op jit(solution)/shard_map/while/body/eval_jaxpr/ppermute | solution.py:33
  289.9 0.6 fusion.70
  290.9 1.0 select_convert_fusion
  292.0 0.7 copy.207
  293.1 2.1 scatter_custom_fusion
  (208 shorter events, 38.2 us)
Async XLA Ops:
  0.7 0.7 copy-start.4
  1.5 0.7 copy-start.2
  4.6 14.0 %copy-start = (bf16[1,1,512,256]{3,2,1,0:T(8,128)(2,1)S(1)}, bf16[1,1,512,256]{3,2,1,0:T(8,128)(2,1)}, u32[]{:S(2)}) copy-start(bf16[1,1,512,256]{3,2,1,0:T(8,128)(2,1)} %param.11) | copy-start | bytes 786436
  19.5 0.7 copy-start.3
  41.7 250.2 %all-to-all-start = ((bf16[32,2,8,1,512]{4,2,1,3,0:T(8,128)(2,1)}), bf16[32,2,8,1,512]{4,2,1,3,0:T(8,128)(2,1)S(1)}, u32[]{:S(2)}, u32[]{:S(2)}) async-start(bf16[32,2,8,1,512]{4,2,1,3,0:T(8,128)(2,1)} %constant_dynamic-update-slice_fusion), calls=%async_computation | async-start | bytes 1048576 | tf_op jit(solution)/shard_map/all_to_all | solution.py:21
  58.1 1.0 copy-start.1
  63.9 33.0 %collective-permute-start = (bf16[2,512,256]{1,2,0:T(8,128)(2,1)S(1)}, bf16[2,512,256]{1,2,0:T(8,128)(2,1)S(1)}, u32[]{:S(2)}, u32[]{:S(2)}) collective-permute-start(bf16[2,512,256]{1,2,0:T(8,128)(2,1)S(1)} %get-tuple-element.428), channel_id=1, source_target_pairs={{0,4},{1,5},{2,6},{3,7},{4,8},{5,9},{6,10},{7,11},{8,12},{9,13},{1... | collective-permute-start | bytes 1572872 | tf_op jit(solution)/shard_map/while/body/eval_jaxpr/ppermute | solution.py:33
  100.7 17.3 %collective-permute-start = (bf16[2,512,256]{1,2,0:T(8,128)(2,1)S(1)}, bf16[2,512,256]{1,2,0:T(8,128)(2,1)S(1)}, u32[]{:S(2)}, u32[]{:S(2)}) collective-permute-start(bf16[2,512,256]{1,2,0:T(8,128)(2,1)S(1)} %get-tuple-element.428), channel_id=1, source_target_pairs={{0,4},{1,5},{2,6},{3,7},{4,8},{5,9},{6,10},{7,11},{8,12},{9,13},{1... | collective-permute-start | bytes 1572872 | tf_op jit(solution)/shard_map/while/body/eval_jaxpr/ppermute | solution.py:33
  121.9 36.4 %collective-permute-start = (bf16[2,512,256]{1,2,0:T(8,128)(2,1)S(1)}, bf16[2,512,256]{1,2,0:T(8,128)(2,1)S(1)}, u32[]{:S(2)}, u32[]{:S(2)}) collective-permute-start(bf16[2,512,256]{1,2,0:T(8,128)(2,1)S(1)} %get-tuple-element.428), channel_id=1, source_target_pairs={{0,4},{1,5},{2,6},{3,7},{4,8},{5,9},{6,10},{7,11},{8,12},{9,13},{1... | collective-permute-start | bytes 1572872 | tf_op jit(solution)/shard_map/while/body/eval_jaxpr/ppermute | solution.py:33
  162.0 38.7 %collective-permute-start = (bf16[2,512,256]{1,2,0:T(8,128)(2,1)S(1)}, bf16[2,512,256]{1,2,0:T(8,128)(2,1)S(1)}, u32[]{:S(2)}, u32[]{:S(2)}) collective-permute-start(bf16[2,512,256]{1,2,0:T(8,128)(2,1)S(1)} %get-tuple-element.428), channel_id=1, source_target_pairs={{0,4},{1,5},{2,6},{3,7},{4,8},{5,9},{6,10},{7,11},{8,12},{9,13},{1... | collective-permute-start | bytes 1572872 | tf_op jit(solution)/shard_map/while/body/eval_jaxpr/ppermute | solution.py:33
  204.6 31.0 %collective-permute-start = (bf16[2,512,256]{1,2,0:T(8,128)(2,1)S(1)}, bf16[2,512,256]{1,2,0:T(8,128)(2,1)S(1)}, u32[]{:S(2)}, u32[]{:S(2)}) collective-permute-start(bf16[2,512,256]{1,2,0:T(8,128)(2,1)S(1)} %get-tuple-element.428), channel_id=1, source_target_pairs={{0,4},{1,5},{2,6},{3,7},{4,8},{5,9},{6,10},{7,11},{8,12},{9,13},{1... | collective-permute-start | bytes 1572872 | tf_op jit(solution)/shard_map/while/body/eval_jaxpr/ppermute | solution.py:33
  239.3 28.7 %collective-permute-start = (bf16[2,512,256]{1,2,0:T(8,128)(2,1)S(1)}, bf16[2,512,256]{1,2,0:T(8,128)(2,1)S(1)}, u32[]{:S(2)}, u32[]{:S(2)}) collective-permute-start(bf16[2,512,256]{1,2,0:T(8,128)(2,1)S(1)} %get-tuple-element.428), channel_id=1, source_target_pairs={{0,4},{1,5},{2,6},{3,7},{4,8},{5,9},{6,10},{7,11},{8,12},{9,13},{1... | collective-permute-start | bytes 1572872 | tf_op jit(solution)/shard_map/while/body/eval_jaxpr/ppermute | solution.py:33
  271.8 13.2 %collective-permute-start = (bf16[2,512,256]{1,2,0:T(8,128)(2,1)S(1)}, bf16[2,512,256]{1,2,0:T(8,128)(2,1)S(1)}, u32[]{:S(2)}, u32[]{:S(2)}) collective-permute-start(bf16[2,512,256]{1,2,0:T(8,128)(2,1)S(1)} %get-tuple-element.428), channel_id=1, source_target_pairs={{0,4},{1,5},{2,6},{3,7},{4,8},{5,9},{6,10},{7,11},{8,12},{9,13},{1... | collective-permute-start | bytes 1572872 | tf_op jit(solution)/shard_map/while/body/eval_jaxpr/ppermute | solution.py:33
